TPU v7x, 32 devices: a whole 2x2x4 slice. The times are simulated.
32 devices in a mesh: section: 2 (over core), hid: 8 (over z, x), mod: 2 (over y).
Axes of the slice: x: 2, y: 2, z: 4, core: 2. Of those that a mesh axis runs over, the one named last changes fastest.
Arguments:
- tokens: float32 [2048, 5120], P(('section', 'hid'), 'mod'), may hold values from -200 to 200
- gain_first: float32 [5120], P('mod'), may hold values from 0.1 to 1.9
- gate_first: bfloat16 [5120, 13824], P('mod', 'hid'), may hold values from -0.078125 to 0.078125
- up_first: bfloat16 [5120, 13824], P('mod', 'hid'), may hold values from -0.078125 to 0.078125
- down_first: bfloat16 [13824, 5120], P('hid', 'mod'), may hold values from -0.0546875 to 0.0546875
- gain_second: float32 [5120], P('mod'), may hold values from 0.1 to 1.9
- gate_second: bfloat16 [5120, 13824], P('mod', ('section', 'hid')), may hold values from -0.078125 to 0.078125
- up_second: bfloat16 [5120, 13824], P('mod', ('section', 'hid')), may hold values from -0.078125 to 0.078125
- down_second: bfloat16 [13824, 5120], P(('section', 'hid'), 'mod'), may hold values from -0.0546875 to 0.0546875
Outputs:
- result: float32 [2048, 5120], P(('section', 'hid'), 'mod')
All inputs are finite; a program needn't handle non-finite values.
Results may differ from a plain program's by a relative error of at most 0.006.
Values may be sent and summed in bfloat16 or wider, within the bound.
A program may use at most 128 MiB of HBM per device.

v0:
```python
import jax
import jax.numpy as jnp
from jax import lax
from jax.sharding import PartitionSpec as P

D = 5120
epsilon = 1e-06


def scale_rows(stream, square_sum, gain):
    return (stream * lax.rsqrt(square_sum[:, None] / D + epsilon) * gain).astype(jnp.bfloat16)


def both_products(segment, w_gate, w_up):
    gate_part = jnp.dot(segment, w_gate, preferred_element_type=jnp.float32).astype(jnp.bfloat16)
    up_part = jnp.dot(segment, w_up, preferred_element_type=jnp.float32).astype(jnp.bfloat16)
    return jnp.concatenate([gate_part, up_part], axis=1)


def swiglu(summed, hidden_units):
    return (jax.nn.silu(summed[:, :hidden_units]) * summed[:, hidden_units:]).astype(jnp.bfloat16)


def per_device(
    tokens,
    gain_first,
    gate_first,
    up_first,
    down_first,
    gain_second,
    gate_second,
    up_second,
    down_second,
):
    square_first = lax.psum(jnp.sum(tokens * tokens, axis=1), "mod")
    normed_first = scale_rows(tokens, square_first, gain_first)
    partial_first = both_products(
        lax.all_gather(normed_first, "hid", axis=0, tiled=True), gate_first, up_first
    )
    units_first = gate_first.shape[1]
    summed_first = lax.psum_scatter(
        partial_first.astype(jnp.float32).astype(jnp.bfloat16),
        "mod",
        scatter_dimension=0,
        tiled=True,
    ).astype(jnp.float32)
    activated_first = swiglu(summed_first, units_first)
    terms_first = jnp.dot(
        lax.all_gather(activated_first, "mod", axis=0, tiled=True),
        down_first,
        preferred_element_type=jnp.float32,
    )
    middle = tokens + lax.psum_scatter(
        terms_first.astype(jnp.bfloat16), "hid", scatter_dimension=0, tiled=True
    ).astype(jnp.float32)
    square_second = lax.psum(jnp.sum(middle * middle, axis=1), "mod")
    normed_second = scale_rows(middle, square_second, gain_second)
    partial_second = both_products(
        lax.all_gather(normed_second, ("section", "hid"), axis=0, tiled=True),
        gate_second,
        up_second,
    )
    units_second = gate_second.shape[1]
    summed_second = lax.psum_scatter(
        partial_second.astype(jnp.float32).astype(jnp.bfloat16),
        "mod",
        scatter_dimension=0,
        tiled=True,
    ).astype(jnp.float32)
    activated_second = swiglu(summed_second, units_second)
    terms_second = jnp.dot(
        lax.all_gather(activated_second, "mod", axis=0, tiled=True),
        down_second,
        preferred_element_type=jnp.float32,
    )
    return middle + lax.psum_scatter(
        terms_second.astype(jnp.bfloat16), ("section", "hid"), scatter_dimension=0, tiled=True
    ).astype(jnp.float32)


def solution(mesh):
    in_specs = (
        P(("section", "hid"), "mod"),
        P("mod"),
        P("mod", "hid"),
        P("mod", "hid"),
        P("hid", "mod"),
        P("mod"),
        P("mod", ("section", "hid")),
        P("mod", ("section", "hid")),
        P(("section", "hid"), "mod"),
    )
    out_specs = P(("section", "hid"), "mod")
    return jax.shard_map(
        per_device, mesh=mesh, in_specs=in_specs, out_specs=out_specs, check_vma=False
    )
```

profile of v0, /device:TPU:0, one launch (start us, length us, event | category | flops | bytes accessed | tf_op | source)
XLA Modules:
  0.0 806.3 jit_solution(4746414149843503871)
XLA Ops:
  8.0 5.9 psum.14
  13.9 2.3 multiply_convert_fusion.1
  16.3 87.7 %all-gather.5.cloned.1.call-done = bf16[1024,2560]{1,0:T(8,128)(2,1)} async-done(((bf16[128,2560]{1,0:T(8,128)(2,1)}), bf16[1024,2560]{1,0:T(8,128)(2,1)}) %all-gather.5.cloned.1.call-update) | async-done | bytes 5242896 | tf_op jit(solution)/shard_map/all_gather | solution.py:38
  104.1 14.3 %convolution_convert_fusion.2 = bf16[1024,1728]{0,1:T(8,128)(2,1)S(1)} fusion(bf16[1024,2560]{1,0:T(8,128)(2,1)} %all-gather.5.cloned.1.call-done, bf16[2560,1728]{0,1:T(8,128)(2,1)} %param.12), kind=kOutput, calls=%fused_computation.4 | convolution fusion | flops 9061466112 | bytes 17629184 | tf_op jit(solution)/shard_map/dot_general | solution.py:16
  118.4 13.0 %convolution_convert_fusion.3 = bf16[1024,1728]{0,1:T(8,128)(2,1)} fusion(bf16[1024,2560]{1,0:T(8,128)(2,1)S(1)} %copy-done.4, bf16[2560,1728]{0,1:T(8,128)(2,1)} %param.11), kind=kOutput, calls=%fused_computation.5 | convolution fusion | flops 9061466112 | bytes 17629184 | tf_op jit(solution)/shard_map/dot_general | solution.py:15
  131.4 5.7 pad_maximum_fusion
  137.2 84.0 %reduce-scatter.5.cloned.1.call-done = bf16[512,3456]{0,1:T(8,128)(2,1)} async-done(((bf16[1024,3456]{0,1:T(8,128)(2,1)}), bf16[512,3456]{0,1:T(8,128)(2,1)}) %reduce-scatter.5.cloned.1.call-update) | async-done | bytes 3538960 | tf_op jit(solution)/shard_map/reduce_scatter | solution.py:41
  221.2 3.0 convert_element_type.49
  224.2 2.5 fusion.1
  226.9 49.3 %all-gather.7.cloned.1.call-done = bf16[1024,1728]{0,1:T(8,128)(2,1)} async-done(((bf16[512,1728]{0,1:T(8,128)(2,1)}), bf16[1024,1728]{0,1:T(8,128)(2,1)}) %all-gather.7.cloned.1.call-update) | async-done | bytes 3538960 | tf_op jit(solution)/shard_map/all_gather | solution.py:49
  276.2 15.0 %convolution_convert_fusion.1 = bf16[1024,2560]{1,0:T(8,128)(2,1)} fusion(bf16[1024,1728]{0,1:T(8,128)(2,1)} %all-gather.7.cloned.1.call-done, bf16[1728,2560]{1,0:T(8,128)(2,1)} %param.13), kind=kOutput, calls=%fused_computation.3 | convolution fusion | flops 9062318080 | bytes 17629184 | tf_op jit(solution)/shard_map/dot_general | solution.py:48
  291.3 103.1 %reduce-scatter.7.cloned.1.call-done = bf16[128,2560]{1,0:T(8,128)(2,1)} async-done(((bf16[1024,2560]{1,0:T(8,128)(2,1)}), bf16[128,2560]{1,0:T(8,128)(2,1)}) %reduce-scatter.7.cloned.1.call-update) | async-done | bytes 655376 | tf_op jit(solution)/shard_map/reduce_scatter | solution.py:53
  395.7 4.9 psum.15
  402.8 87.3 %all-gather.9.cloned.1.call-done = bf16[2048,2560]{1,0:T(8,128)(2,1)} async-done(((bf16[128,2560]{1,0:T(8,128)(2,1)}), bf16[2048,2560]{1,0:T(8,128)(2,1)}) %all-gather.9.cloned.1.call-update) | async-done | bytes 10485776 | tf_op jit(solution)/shard_map/all_gather | solution.py:59
  490.1 13.5 %convolution_convert_fusion.4 = bf16[2048,864]{0,1:T(8,128)(2,1)S(1)} fusion(bf16[2048,2560]{1,0:T(8,128)(2,1)} %all-gather.9.cloned.1.call-done, bf16[2560,864]{0,1:T(8,128)(2,1)} %param.16), kind=kOutput, calls=%fused_computation.10 | convolution fusion | flops 9061466112 | bytes 18448384 | tf_op jit(solution)/shard_map/dot_general | solution.py:16
  503.6 12.5 %convolution_convert_fusion.5 = bf16[2048,864]{0,1:T(8,128)(2,1)} fusion(bf16[2048,2560]{1,0:T(8,128)(2,1)S(1)} %copy-done.3, bf16[2560,864]{0,1:T(8,128)(2,1)} %param.15), kind=kOutput, calls=%fused_computation.11 | convolution fusion | flops 9061466112 | bytes 18448384 | tf_op jit(solution)/shard_map/dot_general | solution.py:15
  516.1 6.0 pad_maximum_fusion.1
  522.4 83.8 %reduce-scatter.9.cloned.1.call-done = bf16[1024,1728]{0,1:T(8,128)(2,1)} async-done(((bf16[2048,1728]{0,1:T(8,128)(2,1)}), bf16[1024,1728]{0,1:T(8,128)(2,1)}) %reduce-scatter.9.cloned.1.call-update) | async-done | bytes 3538960 | tf_op jit(solution)/shard_map/reduce_scatter | solution.py:64
  606.2 2.8 convert_element_type.56
  609.1 2.4 fusion
  611.5 49.4 %all-gather.11.cloned.1.call-done = bf16[2048,864]{0,1:T(8,128)(2,1)} async-done(((bf16[1024,864]{0,1:T(8,128)(2,1)}), bf16[2048,864]{0,1:T(8,128)(2,1)}) %all-gather.11.cloned.1.call-update) | async-done | bytes 3538960 | tf_op jit(solution)/shard_map/all_gather | solution.py:72
  661.0 16.5 %convolution_convert_fusion = bf16[2048,2560]{1,0:T(8,128)(2,1)} fusion(bf16[2048,864]{0,1:T(8,128)(2,1)} %all-gather.11.cloned.1.call-done, bf16[864,2560]{1,0:T(8,128)(2,1)} %param.17), kind=kOutput, calls=%fused_computation | convolution fusion | flops 9064939520 | bytes 18448384 | tf_op jit(solution)/shard_map/dot_general | solution.py:71
  677.6 119.6 %reduce-scatter.11.cloned.1.call-done = bf16[128,2560]{1,0:T(8,128)(2,1)} async-done(((bf16[2048,2560]{1,0:T(8,128)(2,1)}), bf16[128,2560]{1,0:T(8,128)(2,1)}) %reduce-scatter.11.cloned.1.call-update) | async-done | bytes 655376 | tf_op jit(solution)/shard_map/reduce_scatter | solution.py:76
  797.2 2.3 convert_add_fusion
  (31 shorter events, 5.8 us)
Async XLA Ops:
  6.5 97.5 %all-gather.5.cloned.1.call-start = ((), (), s32[]{:S(2)}) async-start(), calls=%async_computation.4 | async-start | bytes 5898240 | tf_op jit(solution)/shard_map/all_gather | solution.py:38
  16.3 204.9 %reduce-scatter.5.cloned.1.call-start = ((), (), s32[]{:S(2)}) async-start(), calls=%async_computation.5 | async-start | bytes 10616832 | tf_op jit(solution)/shard_map/reduce_scatter | solution.py:41
  104.1 14.3 %copy-start.4 = (bf16[1024,2560]{1,0:T(8,128)(2,1)S(1)}, bf16[1024,2560]{1,0:T(8,128)(2,1)}, u32[]{:S(2)}) copy-start(bf16[1024,2560]{1,0:T(8,128)(2,1)} %all-gather.5.cloned.1.call-done) | copy-start | bytes 15728644
  137.2 139.0 %all-gather.7.cloned.1.call-start = ((), (), s32[]{:S(2)}) async-start(), calls=%async_computation.6 | async-start | bytes 5308416 | tf_op jit(solution)/shard_map/all_gather | solution.py:49
  226.7 167.6 %reduce-scatter.7.cloned.1.call-start = ((), (), s32[]{:S(2)}) async-start(), calls=%async_computation.7 | async-start | bytes 5898240 | tf_op jit(solution)/shard_map/reduce_scatter | solution.py:53
  291.2 103.2 %copy-start = (f32[128,2560]{1,0:T(8,128)S(1)}, f32[128,2560]{1,0:T(8,128)}, u32[]{:S(2)}) copy-start(f32[128,2560]{1,0:T(8,128)} %param.9) | copy-start | bytes 3932164
  291.2 109.4 %copy-start.2 = (f32[2560]{0:T(1024)S(1)}, f32[2560]{0:T(1024)}, u32[]{:S(2)}) copy-start(f32[2560]{0:T(1024)} %param.14) | copy-start | bytes 30724
  291.2 198.9 %all-gather.9.cloned.1.call-start = ((), (), s32[]{:S(2)}) async-start(), calls=%async_computation.8 | async-start | bytes 11141120 | tf_op jit(solution)/shard_map/all_gather | solution.py:59
  402.8 203.4 %reduce-scatter.9.cloned.1.call-start = ((), (), s32[]{:S(2)}) async-start(), calls=%async_computation.9 | async-start | bytes 10616832 | tf_op jit(solution)/shard_map/reduce_scatter | solution.py:64
  490.1 13.5 %copy-start.3 = (bf16[2048,2560]{1,0:T(8,128)(2,1)S(1)}, bf16[2048,2560]{1,0:T(8,128)(2,1)}, u32[]{:S(2)}) copy-start(bf16[2048,2560]{1,0:T(8,128)(2,1)} %all-gather.9.cloned.1.call-done) | copy-start | bytes 31457284
  522.1 138.9 %all-gather.11.cloned.1.call-start = ((), (), s32[]{:S(2)}) async-start(), calls=%async_computation.10 | async-start | bytes 5308416 | tf_op jit(solution)/shard_map/all_gather | solution.py:72
  611.5 185.7 %reduce-scatter.11.cloned.1.call-start = ((), (), s32[]{:S(2)}) async-start(), calls=%async_computation.11 | async-start | bytes 11141120 | tf_op jit(solution)/shard_map/reduce_scatter | solution.py:76
  677.5 119.6 %copy-start.1 = (bf16[128,2560]{1,0:T(8,128)(2,1)S(1)}, bf16[128,2560]{1,0:T(8,128)(2,1)}, u32[]{:S(2)}) copy-start(bf16[128,2560]{1,0:T(8,128)(2,1)} %reduce-scatter.7.cloned.1.call-done) | copy-start | bytes 1966084
Sparse Core Ops, SparseCore 0:
  16.4 87.6 all-gather.4
  137.3 83.8 reduce-scatter.4
  226.8 49.3 all-gather.6
  291.3 102.9 reduce-scatter.6
  402.9 87.1 all-gather.8
  522.2 83.9 reduce-scatter.8
  611.6 49.3 all-gather.10
  677.7 119.4 reduce-scatter.10
where the time goes:
time: 807 us; the launch traced here: 806 us
  waiting for transfers between devices  664 us (82%)
  matrix products  84.8 us (11%)
  other arithmetic  32.1 us (4%)
  between operations  13.6 us (2%)
  blocking collectives  10.8 us (1%)
    reduce_scatter x1, waiting for transfers between devices, per_device(): lax.psum_scatter(terms_second.astype(jnp.bfloat16), ('section', 'hid'), s...  120 us
    reduce_scatter x1, waiting for transfers between devices, per_device(): lax.psum_scatter(terms_first.astype(jnp.bfloat16), 'hid', scatter_dimensi...  103 us
    all_gather x1, waiting for transfers between devices, per_device(): lax.all_gather(normed_first, 'hid', axis=0, tiled=True)  87.7 us
    all_gather x1, waiting for transfers between devices, per_device(): lax.all_gather(normed_second, ('section', 'hid'), axis=0, tiled=True)  87.3 us
    reduce_scatter x1, waiting for transfers between devices, per_device(): lax.psum_scatter(partial_first.astype(jnp.float32).astype(jnp.bfloat16),...  84 us
    reduce_scatter x1, waiting for transfers between devices, per_device(): lax.psum_scatter(partial_second.astype(jnp.float32).astype(jnp.bfloat16),...  83.8 us
    all_gather x1, waiting for transfers between devices, per_device(): lax.all_gather(activated_second, 'mod', axis=0, tiled=True)  49.4 us
    all_gather x1, waiting for transfers between devices, per_device(): lax.all_gather(activated_first, 'mod', axis=0, tiled=True)  49.3 us
  transfers between devices with their start and end apart: 8, of which 8 were waited for; matrix products, arithmetic and copies ran while one was open for 0% of the time, Pallas kernels for 0%

commit v1 on v0

--- a/solution.py
+++ b/solution.py
@@ -5,6 +5,28 @@
 
 D = 5120
 epsilon = 1e-06
+
+
+def laid_out(blocks, dim):
+    lengths = list(blocks.shape[1:])
+    lengths[dim] *= blocks.shape[0]
+    return jnp.moveaxis(blocks, 0, dim).reshape(lengths)
+
+
+def grow_blocks(x, axis):
+    devices = lax.axis_size(axis)
+    blocks = x[None]
+    for level in range(devices.bit_length() - 1):
+        stride = 1 << level
+        partner_block = lax.ppermute(blocks, axis, [(i, i ^ stride) for i in range(devices)])
+        both = jnp.stack([blocks, partner_block])
+        upper = lax.axis_index(axis) >> level & 1
+        blocks = jnp.where(upper == 0, both, both[::-1]).reshape(-1, *x.shape)
+    return blocks
+
+
+def doubled_up(x, axis, dim):
+    return laid_out(grow_blocks(x, axis), dim)
 
 
 def scale_rows(stream, square_sum, gain):
@@ -34,9 +56,7 @@
 ):
     square_first = lax.psum(jnp.sum(tokens * tokens, axis=1), "mod")
     normed_first = scale_rows(tokens, square_first, gain_first)
-    partial_first = both_products(
-        lax.all_gather(normed_first, "hid", axis=0, tiled=True), gate_first, up_first
-    )
+    partial_first = both_products(doubled_up(normed_first, "hid", 0), gate_first, up_first)
     units_first = gate_first.shape[1]
     summed_first = lax.psum_scatter(
         partial_first.astype(jnp.float32).astype(jnp.bfloat16),

time: 807 us -> 882 us (1.093)
  waiting for transfers between devices: 664 us -> 731 us
    ppermute x0 -> x3, waiting for transfers between devices: none -> 151 us  [grow_blocks(): lax.ppermute(blocks, axis, [(i, i ^ stride) for i in range(devices)])]
    all_gather x1 -> x0, waiting for transfers between devices: 87.7 us -> none  [per_device(): lax.all_gather(normed_first, 'hid', axis=0, tiled=True)]
  transfers between devices with their start and end apart: 8 -> 10, of which waited for: 8 -> 10; matrix products, arithmetic and copies ran while one was open for 0% -> 0% of each run, Pallas kernels for 0% -> 0%
where the time goes in v1:
time: 882 us
  waiting for transfers between devices  731 us (83%)
  matrix products  81.5 us (9%)
  other arithmetic  37.9 us (4%)
  between operations  13.6 us (2%)
  blocking collectives  10.8 us (1%)
    ppermute x3, waiting for transfers between devices, grow_blocks(): lax.ppermute(blocks, axis, [(i, i ^ stride) for i in range(devices)])  151 us
    reduce_scatter x1, waiting for transfers between devices, per_device(): lax.psum_scatter(terms_second.astype(jnp.bfloat16), ('section', 'hid'), s...  120 us
    reduce_scatter x1, waiting for transfers between devices, per_device(): lax.psum_scatter(terms_first.astype(jnp.bfloat16), 'hid', scatter_dimensi...  103 us
    all_gather x1, waiting for transfers between devices, per_device(): lax.all_gather(normed_second, ('section', 'hid'), axis=0, tiled=True)  87.3 us
    reduce_scatter x1, waiting for transfers between devices, per_device(): lax.psum_scatter(partial_first.astype(jnp.float32).astype(jnp.bfloat16),...  86.6 us
    reduce_scatter x1, waiting for transfers between devices, per_device(): lax.psum_scatter(partial_second.astype(jnp.float32).astype(jnp.bfloat16),...  83.8 us
    all_gather x1, waiting for transfers between devices, per_device(): lax.all_gather(activated_second, 'mod', axis=0, tiled=True)  49.5 us
    all_gather x1, waiting for transfers between devices, per_device(): lax.all_gather(activated_first, 'mod', axis=0, tiled=True)  49.3 us
  transfers between devices with their start and end apart: 10, of which 10 were waited for; matrix products, arithmetic and copies ran while one was open for 0% of the time, Pallas kernels for 0%

profile of v1, /device:TPU:0, one launch (start us, length us, event | category | flops | bytes accessed | tf_op | source)
XLA Modules:
  0.0 881.7 jit_solution(5033510767490989031)
XLA Ops:
  8.0 5.9 psum.14
  17.5 13.6 %collective-permute-done = bf16[1,128,2560]{2,1,0:T(8,128)(2,1)S(1)} collective-permute-done((bf16[1,128,2560]{2,1,0:T(8,128)(2,1)S(1)}, bf16[1,128,2560]{2,1,0:T(8,128)(2,1)S(1)}, u32[]{:S(2)}, u32[]{:S(2)}) %collective-permute-start) | collective-permute-done | bytes 655392 | tf_op jit(solution)/shard_map/ppermute | solution.py:21
  34.4 27.2 %collective-permute-done.1 = bf16[2,128,2560]{2,1,0:T(8,128)(2,1)S(1)} collective-permute-done((bf16[2,128,2560]{2,1,0:T(8,128)(2,1)}, bf16[2,128,2560]{2,1,0:T(8,128)(2,1)S(1)}, u32[]{:S(2)}, u32[]{:S(2)}) %collective-permute-start.1) | collective-permute-done | bytes 1310752 | tf_op jit(solution)/shard_map/ppermute | solution.py:21
  62.3 2.6 collective-permute-start.2
  64.9 110.7 %collective-permute-done.2 = bf16[4,128,2560]{2,1,0:T(8,128)(2,1)} collective-permute-done((bf16[4,128,2560]{2,1,0:T(8,128)(2,1)S(1)}, bf16[4,128,2560]{2,1,0:T(8,128)(2,1)}, u32[]{:S(2)}, u32[]{:S(2)}) %collective-permute-start.2) | collective-permute-done | bytes 2621472 | tf_op jit(solution)/shard_map/ppermute | solution.py:21
  178.9 12.0 %convolution_convert_fusion.2 = bf16[1024,1728]{0,1:T(8,128)(2,1)S(1)} fusion(bf16[1024,2560]{1,0:T(8,128)(2,1)S(1)} %bitcast.28, bf16[2560,1728]{0,1:T(8,128)(2,1)} %param.12), kind=kOutput, calls=%fused_computation.7 | convolution fusion | flops 9061466112 | bytes 17629184 | tf_op jit(solution)/shard_map/dot_general | solution.py:38
  190.9 10.8 %convolution_convert_fusion.3 = bf16[1024,1728]{0,1:T(8,128)(2,1)} fusion(bf16[1024,2560]{1,0:T(8,128)(2,1)S(1)} %bitcast.29, bf16[2560,1728]{0,1:T(8,128)(2,1)S(1)} %bitcast.33), kind=kOutput, calls=%fused_computation.8 | convolution fusion | flops 9061466112 | bytes 17629184 | tf_op jit(solution)/shard_map/dot_general | solution.py:37
  201.6 5.7 pad_maximum_fusion
  207.4 86.6 %reduce-scatter.5.cloned.1.call-done = bf16[512,3456]{0,1:T(8,128)(2,1)} async-done(((bf16[1024,3456]{0,1:T(8,128)(2,1)}), bf16[512,3456]{0,1:T(8,128)(2,1)}) %reduce-scatter.5.cloned.1.call-update) | async-done | bytes 3538960 | tf_op jit(solution)/shard_map/reduce_scatter | solution.py:61
  294.0 3.0 convert_element_type.49
  297.0 2.5 fusion.1
  299.7 49.3 %all-gather.4.cloned.1.call-done = bf16[1024,1728]{0,1:T(8,128)(2,1)} async-done(((bf16[512,1728]{0,1:T(8,128)(2,1)}), bf16[1024,1728]{0,1:T(8,128)(2,1)}) %all-gather.4.cloned.1.call-update) | async-done | bytes 3538960 | tf_op jit(solution)/shard_map/all_gather | solution.py:69
  349.0 15.0 %convolution_convert_fusion.1 = bf16[1024,2560]{1,0:T(8,128)(2,1)} fusion(bf16[1024,1728]{0,1:T(8,128)(2,1)} %all-gather.4.cloned.1.call-done, bf16[1728,2560]{1,0:T(8,128)(2,1)} %param.13), kind=kOutput, calls=%fused_computation.4 | convolution fusion | flops 9062318080 | bytes 17629184 | tf_op jit(solution)/shard_map/dot_general | solution.py:68
  364.1 103.1 %reduce-scatter.7.cloned.1.call-done = bf16[128,2560]{1,0:T(8,128)(2,1)} async-done(((bf16[1024,2560]{1,0:T(8,128)(2,1)}), bf16[128,2560]{1,0:T(8,128)(2,1)}) %reduce-scatter.7.cloned.1.call-update) | async-done | bytes 655376 | tf_op jit(solution)/shard_map/reduce_scatter | solution.py:73
  468.5 4.9 psum.15
  475.7 87.3 %all-gather.6.cloned.1.call-done = bf16[2048,2560]{1,0:T(8,128)(2,1)} async-done(((bf16[128,2560]{1,0:T(8,128)(2,1)}), bf16[2048,2560]{1,0:T(8,128)(2,1)}) %all-gather.6.cloned.1.call-update) | async-done | bytes 10485776 | tf_op jit(solution)/shard_map/all_gather | solution.py:79
  562.9 14.8 %convolution_convert_fusion.4 = bf16[2048,864]{0,1:T(8,128)(2,1)} fusion(bf16[2048,2560]{1,0:T(8,128)(2,1)} %all-gather.6.cloned.1.call-done, bf16[2560,864]{0,1:T(8,128)(2,1)} %param.16), kind=kOutput, calls=%fused_computation.13 | convolution fusion | flops 9061466112 | bytes 18448384 | tf_op jit(solution)/shard_map/dot_general | solution.py:38
  577.7 12.4 %convolution_convert_fusion.5 = bf16[2048,864]{0,1:T(8,128)(2,1)} fusion(bf16[2048,2560]{1,0:T(8,128)(2,1)S(1)} %copy-done.3, bf16[2560,864]{0,1:T(8,128)(2,1)} %param.15), kind=kOutput, calls=%fused_computation.14 | convolution fusion | flops 9061466112 | bytes 18448384 | tf_op jit(solution)/shard_map/dot_general | solution.py:37
  590.1 7.3 pad_maximum_fusion.1
  597.7 83.8 %reduce-scatter.9.cloned.1.call-done = bf16[1024,1728]{0,1:T(8,128)(2,1)} async-done(((bf16[2048,1728]{0,1:T(8,128)(2,1)}), bf16[1024,1728]{0,1:T(8,128)(2,1)}) %reduce-scatter.9.cloned.1.call-update) | async-done | bytes 3538960 | tf_op jit(solution)/shard_map/reduce_scatter | solution.py:84
  681.6 2.8 convert_element_type.56
  686.9 49.5 %all-gather.8.cloned.1.call-done = bf16[2048,864]{0,1:T(8,128)(2,1)} async-done(((bf16[1024,864]{0,1:T(8,128)(2,1)}), bf16[2048,864]{0,1:T(8,128)(2,1)}) %all-gather.8.cloned.1.call-update) | async-done | bytes 3538960 | tf_op jit(solution)/shard_map/all_gather | solution.py:92
  736.3 16.5 %convolution_convert_fusion = bf16[2048,2560]{1,0:T(8,128)(2,1)} fusion(bf16[2048,864]{0,1:T(8,128)(2,1)} %all-gather.8.cloned.1.call-done, bf16[864,2560]{1,0:T(8,128)(2,1)} %param.17), kind=kOutput, calls=%fused_computation | convolution fusion | flops 9064939520 | bytes 18448384 | tf_op jit(solution)/shard_map/dot_general | solution.py:91
  752.8 119.6 %reduce-scatter.11.cloned.1.call-done = bf16[128,2560]{1,0:T(8,128)(2,1)} async-done(((bf16[2048,2560]{1,0:T(8,128)(2,1)}), bf16[128,2560]{1,0:T(8,128)(2,1)}) %reduce-scatter.11.cloned.1.call-update) | async-done | bytes 655376 | tf_op jit(solution)/shard_map/reduce_scatter | solution.py:96
  (45 shorter events, 21.3 us)
Async XLA Ops:
  6.5 287.5 %reduce-scatter.5.cloned.1.call-start = ((), (), s32[]{:S(2)}) async-start(), calls=%async_computation.4 | async-start | bytes 10616832 | tf_op jit(solution)/shard_map/reduce_scatter | solution.py:61
  15.5 15.7 %collective-permute-start = (bf16[1,128,2560]{2,1,0:T(8,128)(2,1)S(1)}, bf16[1,128,2560]{2,1,0:T(8,128)(2,1)S(1)}, u32[]{:S(2)}, u32[]{:S(2)}) collective-permute-start(bf16[1,128,2560]{2,1,0:T(8,128)(2,1)S(1)} %get-tuple-element.6), channel_id=1, source_target_pairs={{0,2},{2,0},{4,6},{6,4},{8,10},{10,8},{12,14},{14,12},{1,3},{3,1},... | collective-permute-start | bytes 1966088 | tf_op jit(solution)/shard_map/ppermute | solution.py:21
  32.6 29.0 %collective-permute-start.1 = (bf16[2,128,2560]{2,1,0:T(8,128)(2,1)}, bf16[2,128,2560]{2,1,0:T(8,128)(2,1)S(1)}, u32[]{:S(2)}, u32[]{:S(2)}) collective-permute-start(bf16[2,128,2560]{2,1,0:T(8,128)(2,1)} %get-tuple-element.8), channel_id=1, source_target_pairs={{0,4},{2,6},{4,0},{6,2},{8,12},{10,14},{12,8},{14,10},{1,5},{3,7},... | collective-permute-start | bytes 3932168 | tf_op jit(solution)/shard_map/ppermute | solution.py:21
  62.3 113.3 %collective-permute-start.2 = (bf16[4,128,2560]{2,1,0:T(8,128)(2,1)S(1)}, bf16[4,128,2560]{2,1,0:T(8,128)(2,1)}, u32[]{:S(2)}, u32[]{:S(2)}) collective-permute-start(bf16[4,128,2560]{2,1,0:T(8,128)(2,1)S(1)} %bitcast.26), channel_id=1, source_target_pairs={{0,8},{2,10},{4,12},{6,14},{8,0},{10,2},{12,4},{14,6},{1,9},{3,11}... | collective-permute-start | bytes 7864328 | tf_op jit(solution)/shard_map/ppermute | solution.py:21
  177.8 13.1 %slice-start = ((s8[8847360]{0:T(1024)(128)(4,1)}), s8[458752]{0:T(1024)(128)(4,1)S(1)}, s32[]{:S(2)}) async-start(s8[8847360]{0:T(1024)(128)(4,1)} %bitcast.32), calls=%async_computation.11 | async-start | bytes 917504
  178.8 12.0 %slice-start.1 = ((s8[8847360]{0:T(1024)(128)(4,1)}), s8[4194304]{0:T(1024)(128)(4,1)S(1)}, s32[]{:S(2)}) async-start(s8[8847360]{0:T(1024)(128)(4,1)} %bitcast.32), calls=%async_computation.12 | async-start | bytes 8388608
  178.9 12.0 %slice-start.2 = ((s8[8847360]{0:T(1024)(128)(4,1)}), s8[4194304]{0:T(1024)(128)(4,1)S(1)}, s32[]{:S(2)}) async-start(s8[8847360]{0:T(1024)(128)(4,1)} %bitcast.32), calls=%async_computation.13 | async-start | bytes 8388608
  207.4 141.6 %all-gather.4.cloned.1.call-start = ((), (), s32[]{:S(2)}) async-start(), calls=%async_computation.5 | async-start | bytes 5308416 | tf_op jit(solution)/shard_map/all_gather | solution.py:69
  299.5 167.7 %reduce-scatter.7.cloned.1.call-start = ((), (), s32[]{:S(2)}) async-start(), calls=%async_computation.6 | async-start | bytes 5898240 | tf_op jit(solution)/shard_map/reduce_scatter | solution.py:73
  364.0 103.2 %copy-start = (f32[128,2560]{1,0:T(8,128)S(1)}, f32[128,2560]{1,0:T(8,128)}, u32[]{:S(2)}) copy-start(f32[128,2560]{1,0:T(8,128)} %param.9) | copy-start | bytes 3932164
  364.0 109.5 %copy-start.2 = (f32[2560]{0:T(1024)S(1)}, f32[2560]{0:T(1024)}, u32[]{:S(2)}) copy-start(f32[2560]{0:T(1024)} %param.14) | copy-start | bytes 30724
  364.0 198.9 %all-gather.6.cloned.1.call-start = ((), (), s32[]{:S(2)}) async-start(), calls=%async_computation.7 | async-start | bytes 11141120 | tf_op jit(solution)/shard_map/all_gather | solution.py:79
  475.6 205.9 %reduce-scatter.9.cloned.1.call-start = ((), (), s32[]{:S(2)}) async-start(), calls=%async_computation.8 | async-start | bytes 10616832 | tf_op jit(solution)/shard_map/reduce_scatter | solution.py:84
  562.9 14.8 %copy-start.3 = (bf16[2048,2560]{1,0:T(8,128)(2,1)S(1)}, bf16[2048,2560]{1,0:T(8,128)(2,1)}, u32[]{:S(2)}) copy-start(bf16[2048,2560]{1,0:T(8,128)(2,1)} %all-gather.6.cloned.1.call-done) | copy-start | bytes 31457284
  597.5 138.8 %all-gather.8.cloned.1.call-start = ((), (), s32[]{:S(2)}) async-start(), calls=%async_computation.9 | async-start | bytes 5308416 | tf_op jit(solution)/shard_map/all_gather | solution.py:92
  686.8 185.7 %reduce-scatter.11.cloned.1.call-start = ((), (), s32[]{:S(2)}) async-start(), calls=%async_computation.10 | async-start | bytes 11141120 | tf_op jit(solution)/shard_map/reduce_scatter | solution.py:96
  752.8 119.7 %copy-start.1 = (bf16[128,2560]{1,0:T(8,128)(2,1)S(1)}, bf16[128,2560]{1,0:T(8,128)(2,1)}, u32[]{:S(2)}) copy-start(bf16[128,2560]{1,0:T(8,128)(2,1)} %reduce-scatter.7.cloned.1.call-done) | copy-start | bytes 1966084
Sparse Core Ops, SparseCore 0:
  207.5 86.4 reduce-scatter.4
  299.6 49.3 all-gather.3
  364.2 102.9 reduce-scatter.6
  475.8 87.1 all-gather.5
  597.6 83.9 reduce-scatter.8
  686.9 49.3 all-gather.7
  753.0 119.4 reduce-scatter.10
